TPU v7x, 32 devices: a whole 2x2x4 slice. The times are simulated.
32 devices in a mesh: row: 8 (over z, core), col: 4 (over y, x).
Axes of the slice: x: 2, y: 2, z: 4, core: 2. Of those that a mesh axis runs over, the one named last changes fastest.
Arguments:
- patches: bfloat16 [8, 4, 2, 16, 128, 128], P('row', 'col'), as said below
- windows: bfloat16 [8, 4, 2, 16, 36864], P('row', 'col'), as said below
- candidates: int32 [8, 4, 2, 2, 128], P('row', 'col'), may hold values from -32 to 32, as said below
- live: int32 [8, 4, 2], replicated, may hold values from 1 to 16, as said below
- edges: int32 [8, 2, 2820], P('row', None, 'col'), may hold values from 0 to 255, as said below
- stiffness: float32 [8, 2820], P('row', 'col'), may hold values from 0.3 to 3
Outputs:
- matches: float32 [8, 4, 2, 3, 16], P('row', 'col')
- mesh_shift: float32 [8, 4, 2, 256], P('row', 'col')
Inputs may be any that keep to these rules, and one draw needn't show every extreme that they name: `candidates`: the candidate shifts of a patch need not be distinct. live[r, c, k] counts the live slots of seam k of tile (r, c): slots 0 to live - 1; the same for all devices. Each tile's springs are the edges of its 16 x 16 vertex grid, horizontal and vertical, and one diagonal of every cell, in any order. `windows`: window k of tile (r, c) serves the seam that tile (r, c-1) (k = 0) or tile (r-1, c) (k = 1) holds as its seam k. `patches`: patch p of seam k is scored against window p of the neighbour.
All inputs are finite; a program needn't handle non-finite values.
Results may differ from a plain program's by a relative error of at most 0.0003.
Values may be sent and summed in bfloat16 or wider, within the bound.
A program may use at most 64 MiB of HBM per device.

v0:
```python
import jax
import jax.numpy as jnp
from jax import lax
from jax.sharding import PartitionSpec as P

REACH = 32
WIN = 192
NS = 8
P_SIZE = 16
BLK = 4
GV = 16
ITERS = 3
LAMBDA_REG = 0.05
EPSILON = 1e-05
PRECISE = lax.Precision.HIGHEST


def shifted(x, axis, by):
    length = lax.axis_size(axis)
    pairs = [(i, i + by) for i in range(length) if 0 <= i + by < length]
    return lax.ppermute(x, axis, pairs)


def with_halo(block, sides, width):
    for axis, dim in sides:
        count = lax.axis_size(axis)
        forward = [(i, i + 1) for i in range(count - 1)]
        backward = [(target, source) for source, target in forward]
        low = lax.ppermute(
            lax.slice_in_dim(block, block.shape[dim] - width, None, axis=dim), axis, forward
        )
        high = lax.ppermute(lax.slice_in_dim(block, 0, width, axis=dim), axis, backward)
        block = jnp.concatenate([low, block, high], axis=dim)
    return block


def match_block(patch_raw, frames, list_y, list_x):
    patch_size = patch_raw.shape[-1]
    cand_count = list_y.shape[-1]
    pixel_count = float(patch_size * patch_size)
    frame_pixels_all = frames.reshape(frames.shape[0], WIN, WIN)

    def crop_all(frame_pixels, shifts_y, shifts_x):

        def crop_one(move_y, move_x):
            return lax.dynamic_slice(
                frame_pixels, (REACH + move_y, REACH + move_x), (patch_size, patch_size)
            )

        return jax.vmap(crop_one)(shifts_y, shifts_x)

    cropped = jax.vmap(crop_all)(frame_pixels_all, list_y, list_x)
    unit_plane = jnp.ones((patch_size, patch_size), patch_raw.dtype)
    patch_sum = jnp.einsum("byx,yx->b", patch_raw, unit_plane, preferred_element_type=jnp.float32)
    patch_square = jnp.einsum(
        "byx,byx->b", patch_raw, patch_raw, preferred_element_type=jnp.float32
    )
    crop_sum = jnp.einsum("bsyx,yx->bs", cropped, unit_plane, preferred_element_type=jnp.float32)
    crop_square = jnp.einsum("bsyx,bsyx->bs", cropped, cropped, preferred_element_type=jnp.float32)
    cross_sum = jnp.einsum("byx,bsyx->bs", patch_raw, cropped, preferred_element_type=jnp.float32)
    patch_mean = patch_sum / pixel_count
    crop_mean = crop_sum / pixel_count
    patch_var = patch_square / pixel_count - patch_mean * patch_mean
    crop_var = crop_square / pixel_count - crop_mean * crop_mean
    cross_mean = cross_sum / pixel_count - patch_mean[:, None] * crop_mean
    correl = cross_mean / jnp.sqrt((patch_var[:, None] + EPSILON) * (crop_var + EPSILON))
    weight = (1.5 + correl) * (1.5 + correl)
    weight_sum = jnp.sum(weight, axis=1)
    along_y = jnp.sum(weight * list_y.astype(jnp.float32), axis=1) / (REACH * weight_sum)
    along_x = jnp.sum(weight * list_x.astype(jnp.float32), axis=1) / (REACH * weight_sum)
    return jnp.stack([along_y, along_x, weight_sum / cand_count])


def match_strip(patch_raw, frames, shift_list, live_count):
    shifts = shift_list.reshape(2, P_SIZE, NS)
    blocks = (live_count + BLK - 1) // BLK

    def one_block(block_index, result):
        block_start = (block_index * BLK).astype(jnp.int32)
        scored = match_block(
            lax.dynamic_slice_in_dim(patch_raw, block_start, BLK, 0),
            lax.dynamic_slice_in_dim(frames, block_start, BLK, 0),
            lax.dynamic_slice_in_dim(shifts[0], block_start, BLK, 0),
            lax.dynamic_slice_in_dim(shifts[1], block_start, BLK, 0),
        )
        return lax.dynamic_update_slice(result, scored, (jnp.zeros((), jnp.int32), block_start))

    result = lax.fori_loop(0, blocks, one_block, jnp.zeros((3, P_SIZE), jnp.float32))
    keeper = (jnp.arange(P_SIZE) < live_count).astype(jnp.float32)
    return result * keeper


def body(patches, windows, candidates, live, edges, stiffness):
    tile_row = lax.axis_index("row")
    tile_col = lax.axis_index("col")
    last_row = lax.axis_size("row") - 1
    last_col = lax.axis_size("col") - 1
    far_east = shifted(windows[0, 0, 0], "col", -1)
    far_south = shifted(windows[0, 0, 1], "row", -1)
    count_east = jnp.where(tile_col < last_col, live[tile_row, tile_col, 0], 0)
    count_south = jnp.where(tile_row < last_row, live[tile_row, tile_col, 1], 0)
    own_east = match_strip(patches[0, 0, 0], far_east, candidates[0, 0, 0], count_east)
    own_south = match_strip(patches[0, 0, 1], far_south, candidates[0, 0, 1], count_south)
    from_west = shifted(own_east, "col", 1)
    from_north = shifted(own_south, "row", 1)
    matches = jnp.stack([own_east, own_south])[None, None]
    slots = jnp.arange(P_SIZE)
    picker = (jnp.arange(GV)[None, :] == (slots * GV // P_SIZE)[:, None]).astype(jnp.float32)
    vertex = jnp.arange(GV * GV)
    incidence = (edges[0, 0][:, None] == vertex[None, :]).astype(jnp.float32) - (
        edges[0, 1][:, None] == vertex[None, :]
    ).astype(jnp.float32)
    spring = stiffness[0]

    def spread(values):
        return jnp.dot(values, picker, precision=PRECISE)

    def sample(values):
        return jnp.dot(values, picker.T, precision=PRECISE)

    conf_east = own_east[2]
    conf_south = own_south[2]
    conf_west = from_west[2]
    conf_north = from_north[2]

    def operate(vector):
        border = with_halo(vector, (("row", 1), ("col", 2)), 1)
        flat_field = vector.reshape(2, GV * GV)
        stretch = jnp.dot(flat_field, incidence.T, precision=PRECISE) * spring
        output = (LAMBDA_REG * flat_field + jnp.dot(stretch, incidence, precision=PRECISE)).reshape(
            2, GV, GV
        )
        output = output.at[:, :, GV - 1].add(
            spread(conf_east * sample(vector[:, :, GV - 1] - border[:, 1:-1, -1]))
        )
        output = output.at[:, :, 0].add(
            spread(conf_west * sample(vector[:, :, 0] - border[:, 1:-1, 0]))
        )
        output = output.at[:, GV - 1, :].add(
            spread(conf_south * sample(vector[:, GV - 1, :] - border[:, -1, 1:-1]))
        )
        output = output.at[:, 0, :].add(
            spread(conf_north * sample(vector[:, 0, :] - border[:, 0, 1:-1]))
        )
        return output

    forcing = jnp.zeros((2, GV, GV), jnp.float32)
    forcing = forcing.at[:, :, GV - 1].add(spread(conf_east * own_east[:2]))
    forcing = forcing.at[:, :, 0].add(-spread(conf_west * from_west[:2]))
    forcing = forcing.at[:, GV - 1, :].add(spread(conf_south * own_south[:2]))
    forcing = forcing.at[:, 0, :].add(-spread(conf_north * from_north[:2]))
    solution = jnp.zeros_like(forcing)
    residual = forcing

    def two_products(values, applied):
        return lax.psum((jnp.sum(values * values), jnp.sum(values * applied)), ("row", "col"))

    applied = operate(residual)
    norm_now, product = two_products(residual, applied)
    step_length = norm_now / product
    direction = residual
    along = applied
    for iteration in range(ITERS):
        solution = solution + step_length * direction
        residual = residual - step_length * along
        if iteration + 1 < ITERS:
            applied = operate(residual)
            norm_next, product = two_products(residual, applied)
            beta_ratio = norm_next / norm_now
            step_length = norm_next / (product - beta_ratio * norm_next / step_length)
            direction = residual + beta_ratio * direction
            along = applied + beta_ratio * along
            norm_now = norm_next
    mesh_shift = solution.reshape(2, GV * GV)[None, None]
    return (matches, mesh_shift)


def solution(mesh):
    return jax.shard_map(
        body,
        mesh=mesh,
        in_specs=(
            P("row", "col", None, None, None, None),
            P("row", "col", None, None, None),
            P("row", "col", None, None, None),
            P(),
            P("row", None, "col"),
            P("row", "col"),
        ),
        out_specs=(P("row", "col", None, None, None), P("row", "col", None, None)),
        check_vma=False,
    )
```

profile of v0, /device:TPU:0, one launch (start us, length us, event | category | flops | bytes accessed | tf_op | source)
XLA Modules:
  0.0 767.8 jit_solution(11452853252674101553)
XLA Ops:
  0.7 2.9 slice_bitcast_fusion.1
  12.0 91.7 %while.49 = (s32[]{:T(128)}, f32[3,16]{1,0:T(4,128)S(1)}, s32[]{:T(128)}, bf16[16,128,128]{2,1,0:T(8,128)(2,1)S(1)}, bf16[16,36864]{1,0:T(8,128)(2,1)}, /*index=...) while((s32[]{:T(128)}, f32[3,16]{1,0:T(4,128)S(1)}, ...), condition=%wide.region_9.10_spmd, body=%wide.region_5.9_spmd.sunk | while | flops 5178357 | bytes 5322758 | solution.py:88
  14.3 87.7 %while.51 = (s32[]{:T(128)}, bf16[4,192,192]{2,1,0:T(8,128)(2,1)S(1)}, s32[32,3]{0,1:T(4,128)S(1)}, bf16[32,128,128]{2,1,0:T(8,128)(2,1)S(1)}, s32[]{:T(128)}) while((s32[]{:T(128)}, bf16[4,192,192]{2,1,0:T(8,128)(2,1)S(1)}, s32[32,3]{0,1:T(4,128)S(1)}, bf16[32,128,128]{2,1,0:T(8,128)(2,1)S(1)}, s32[]{:T(128)}) %tuple.207), condition=%wide.while_cond.17, body=%wide.while_body.17.sunk | while | flops 2 | bytes 65665 | solution.py:46
  15.0 2.0 dynamic-slice_dynamic-update-slice_fusion.4
  17.7 2.0 dynamic-slice_dynamic-update-slice_fusion.4
  20.4 2.0 dynamic-slice_dynamic-update-slice_fusion.4
  23.2 2.0 dynamic-slice_dynamic-update-slice_fusion.4
  25.9 2.0 dynamic-slice_dynamic-update-slice_fusion.4
  28.7 2.0 dynamic-slice_dynamic-update-slice_fusion.4
  31.4 2.0 dynamic-slice_dynamic-update-slice_fusion.4
  34.1 2.0 dynamic-slice_dynamic-update-slice_fusion.4
  36.9 2.0 dynamic-slice_dynamic-update-slice_fusion.4
  39.6 2.0 dynamic-slice_dynamic-update-slice_fusion.4
  42.4 2.0 dynamic-slice_dynamic-update-slice_fusion.4
  45.1 2.0 dynamic-slice_dynamic-update-slice_fusion.4
  47.8 2.0 dynamic-slice_dynamic-update-slice_fusion.4
  50.6 2.0 dynamic-slice_dynamic-update-slice_fusion.4
  53.3 2.0 dynamic-slice_dynamic-update-slice_fusion.4
  56.1 2.0 dynamic-slice_dynamic-update-slice_fusion.4
  58.8 2.0 dynamic-slice_dynamic-update-slice_fusion.4
  61.5 2.0 dynamic-slice_dynamic-update-slice_fusion.4
  64.3 2.0 dynamic-slice_dynamic-update-slice_fusion.4
  67.0 2.0 dynamic-slice_dynamic-update-slice_fusion.4
  69.8 2.0 dynamic-slice_dynamic-update-slice_fusion.4
  72.5 2.0 dynamic-slice_dynamic-update-slice_fusion.4
  75.2 2.0 dynamic-slice_dynamic-update-slice_fusion.4
  78.0 2.0 dynamic-slice_dynamic-update-slice_fusion.4
  80.7 2.0 dynamic-slice_dynamic-update-slice_fusion.4
  83.5 2.0 dynamic-slice_dynamic-update-slice_fusion.4
  86.2 2.0 dynamic-slice_dynamic-update-slice_fusion.4
  88.9 2.0 dynamic-slice_dynamic-update-slice_fusion.4
  91.7 2.0 dynamic-slice_dynamic-update-slice_fusion.4
  94.4 2.0 dynamic-slice_dynamic-update-slice_fusion.4
  97.1 2.0 dynamic-slice_dynamic-update-slice_fusion.4
  99.9 2.0 dynamic-slice_dynamic-update-slice_fusion.4
  103.7 12.8 %collective-permute-start.3 = (f32[3,16]{1,0:T(4,128)S(1)}, f32[3,16]{1,0:T(4,128)S(1)}, u32[]{:S(2)}, u32[]{:S(2)}) collective-permute-start(f32[3,16]{1,0:T(4,128)S(1)} %broadcast_multiply_fusion.2), channel_id=1, source_target_pairs={{0,4},{4,8},{8,12},{12,16},{16,20},{20,24},{24,28},{1,5},{5,9},{9,... | collective-permute-start | bytes 584 | tf_op jit(solution)/shard_map/ppermute | solution.py:21
  116.6 88.6 %while.47 = (s32[]{:T(128)}, f32[3,16]{1,0:T(4,128)S(1)}, s32[]{:T(128)}, bf16[16,128,128]{2,1,0:T(8,128)(2,1)S(1)}, bf16[16,36864]{1,0:T(8,128)(2,1)}, /*index=...) while((s32[]{:T(128)}, f32[3,16]{1,0:T(4,128)S(1)}, ...), condition=%wide.region_4.5_spmd, body=%wide.region_0.4_spmd.sunk | while | flops 5178357 | bytes 5314510 | solution.py:88
  118.5 85.1 %while.50 = (s32[]{:T(128)}, bf16[4,192,192]{2,1,0:T(8,128)(2,1)S(1)}, s32[32,3]{0,1:T(4,128)S(1)}, bf16[32,128,128]{2,1,0:T(8,128)(2,1)S(1)}, s32[]{:T(128)}) while((s32[]{:T(128)}, bf16[4,192,192]{2,1,0:T(8,128)(2,1)S(1)}, s32[32,3]{0,1:T(4,128)S(1)}, bf16[32,128,128]{2,1,0:T(8,128)(2,1)S(1)}, s32[]{:T(128)}) %tuple.210), condition=%wide.while_cond.16, body=%wide.while_body.16.sunk | while | flops 2 | bytes 65665 | solution.py:46
  205.3 183.9 %collective-permute-start.2 = (f32[3,16]{1,0:T(4,128)S(1)}, f32[3,16]{1,0:T(4,128)S(1)}, u32[]{:S(2)}, u32[]{:S(2)}) collective-permute-start(f32[3,16]{1,0:T(4,128)S(1)} %broadcast_multiply_fusion.3), channel_id=1, source_target_pairs={{0,1},{1,2},{2,3},{4,5},{5,6},{6,7},{8,9},{9,10},{10,11},{12,13},{... | collective-permute-start | bytes 584 | tf_op jit(solution)/shard_map/ppermute | solution.py:21
  395.5 3.4 collective-permute-start.4
  401.7 184.5 %collective-permute-start.7 = (f32[2,18,1]{1,0,2:T(2,128)S(1)}, f32[2,18,1]{1,0,2:T(2,128)S(1)}, u32[]{:S(2)}, u32[]{:S(2)}) collective-permute-start(f32[2,18,1]{1,0,2:T(2,128)S(1)} %get-tuple-element.508), channel_id=1, source_target_pairs={{0,1},{1,2},{2,3},{4,5},{5,6},{6,7},{8,9},{9,10},{10,11},{12,13},{... | collective-permute-start | bytes 440 | tf_op jit(solution)/shard_map/ppermute | solution.py:29
  590.0 43.7 %all-reduce.3 = (f32[]{:T(128)}, f32[]{:T(128)}) all-reduce(f32[]{:T(128)} %get-tuple-element.427, f32[]{:T(128)} %get-tuple-element.426), channel_id=1, replica_groups=mesh['row'=8,'col'=4] {'row','col'}, use_global_device_ids=true, to_apply=%region_11.12 | all-reduce | flops 2 | bytes 16 | tf_op jit(solution)/shard_map/psum | solution.py:156
  640.1 3.5 collective-permute-done.9
  645.7 4.8 collective-permute-start.11
  654.6 43.1 %all-reduce.2 = (f32[]{:T(128)}, f32[]{:T(128)}) all-reduce(f32[]{:T(128)} %get-tuple-element.425, f32[]{:T(128)} %get-tuple-element.424), channel_id=1, replica_groups=mesh['row'=8,'col'=4] {'row','col'}, use_global_device_ids=true, to_apply=%region_15.16 | all-reduce | flops 2 | bytes 16 | tf_op jit(solution)/shard_map/psum | solution.py:156
  707.2 2.2 collective-permute-done.13
  711.5 4.8 collective-permute-start.15
  720.1 43.0 %all-reduce.1 = (f32[]{:T(128)}, f32[]{:T(128)}) all-reduce(f32[]{:T(128)} %get-tuple-element.423, f32[]{:T(128)} %get-tuple-element.422), channel_id=1, replica_groups=mesh['row'=8,'col'=4] {'row','col'}, use_global_device_ids=true, to_apply=%region_19.20 | all-reduce | flops 2 | bytes 16 | tf_op jit(solution)/shard_map/psum | solution.py:156
  (364 shorter events, 156.0 us)
Async XLA Ops:
  0.6 8.2 %copy-start.10 = (s32[1,1,2,2,128]{4,3,2,1,0:T(2,128)S(1)}, s32[1,1,2,2,128]{4,3,2,1,0:T(2,128)}, u32[]{:S(2)}) copy-start(s32[1,1,2,2,128]{4,3,2,1,0:T(2,128)} %param.44) | copy-start | bytes 6148
  0.6 8.4 %copy-start.7 = (f32[1,705]{1,0:T(1,128)S(1)}, f32[1,705]{1,0:T(1,128)}, u32[]{:S(2)}) copy-start(f32[1,705]{1,0:T(1,128)} %param.47) | copy-start | bytes 8464
  0.7 10.6 %copy-start.3 = (s32[1,2,705]{2,1,0:T(2,128)S(1)}, s32[1,2,705]{2,1,0:T(2,128)}, u32[]{:S(2)}) copy-start(s32[1,2,705]{2,1,0:T(2,128)} %param.46) | copy-start | bytes 16924
  0.7 11.2 %copy-start = (bf16[1,1,2,16,128,128]{5,4,3,2,1,0:T(8,128)(2,1)S(1)}, bf16[1,1,2,16,128,128]{5,4,3,2,1,0:T(8,128)(2,1)}, u32[]{:S(2)}) copy-start(bf16[1,1,2,16,128,128]{5,4,3,2,1,0:T(8,128)(2,1)} %param.42) | copy-start | bytes 3145732
  3.6 8.4 %collective-permute-start.1 = (bf16[16,36864]{1,0:T(8,128)(2,1)S(1)}, bf16[16,36864]{1,0:T(8,128)(2,1)}, u32[]{:S(2)}, u32[]{:S(2)}) collective-permute-start(bf16[16,36864]{1,0:T(8,128)(2,1)S(1)} %get-tuple-element.501), channel_id=1, source_target_pairs={{4,0},{8,4},{12,8},{16,12},{20,16},{24,20},{28,24},{5,1},{9,5},{13... | collective-permute-start | bytes 3538952 | tf_op jit(solution)/shard_map/ppermute | solution.py:21
  4.9 111.7 %collective-permute-start = (bf16[16,36864]{1,0:T(8,128)(2,1)}, bf16[16,36864]{1,0:T(8,128)(2,1)}, u32[]{:S(2)}, u32[]{:S(2)}) collective-permute-start(bf16[16,36864]{1,0:T(8,128)(2,1)} %get-tuple-element.500), channel_id=1, source_target_pairs={{1,0},{2,1},{3,2},{5,4},{6,5},{7,6},{9,8},{10,9},{11,10},{13,12},{... | collective-permute-start | bytes 3538952 | tf_op jit(solution)/shard_map/ppermute | solution.py:21
  12.0 91.7 %copy-start.8 = (f32[16]{0:T(128)S(1)}, f32[16]{0:T(128)}, u32[]{:S(2)}) copy-start(f32[16]{0:T(128)} %compare_convert_fusion) | copy-start | bytes 196
  12.0 0.6 copy-start.1
  101.9 1.7 copy-start.2
  103.7 286.6 %collective-permute-start.3 = (f32[3,16]{1,0:T(4,128)S(1)}, f32[3,16]{1,0:T(4,128)S(1)}, u32[]{:S(2)}, u32[]{:S(2)}) collective-permute-start(f32[3,16]{1,0:T(4,128)S(1)} %broadcast_multiply_fusion.2), channel_id=1, source_target_pairs={{0,4},{4,8},{8,12},{12,16},{16,20},{20,24},{24,28},{1,5},{5,9},{9,... | collective-permute-start | bytes 584 | tf_op jit(solution)/shard_map/ppermute | solution.py:21
  116.6 88.7 %copy-start.9 = (f32[16]{0:T(128)S(1)}, f32[16]{0:T(128)}, u32[]{:S(2)}) copy-start(f32[16]{0:T(128)} %compare_convert_fusion.1) | copy-start | bytes 196
  116.6 272.6 %copy-start.11 = (s32[16]{0:T(128)S(1)}, s32[16]{0:T(128)}, u32[]{:S(2)}) copy-start(s32[16]{0:T(128)} %and_select_fusion) | copy-start | bytes 196
  116.6 277.2 %copy-start.4 = (s32[705]{0:T(1024)S(1)}, s32[705]{0:T(1024)}, u32[]{:S(2)}) copy-start(s32[705]{0:T(1024)} %get-tuple-element.428) | copy-start | bytes 8464
  116.6 277.1 %copy-start.5 = (s32[705]{0:T(1024)S(1)}, s32[705]{0:T(1024)}, u32[]{:S(2)}) copy-start(s32[705]{0:T(1024)} %get-tuple-element.429) | copy-start | bytes 8464
  116.6 277.1 %copy-start.6 = (f32[705]{0:T(1024)S(1)}, f32[705]{0:T(1024)}, u32[]{:S(2)}) copy-start(f32[705]{0:T(1024)} %reduce.44) | copy-start | bytes 8464
  205.3 185.3 %collective-permute-start.2 = (f32[3,16]{1,0:T(4,128)S(1)}, f32[3,16]{1,0:T(4,128)S(1)}, u32[]{:S(2)}, u32[]{:S(2)}) collective-permute-start(f32[3,16]{1,0:T(4,128)S(1)} %broadcast_multiply_fusion.3), channel_id=1, source_target_pairs={{0,1},{1,2},{2,3},{4,5},{5,6},{6,7},{8,9},{9,10},{10,11},{12,13},{... | collective-permute-start | bytes 584 | tf_op jit(solution)/shard_map/ppermute | solution.py:21
  392.1 3.3 collective-permute-start.5
  395.5 4.2 collective-permute-start.4
  400.4 185.8 %collective-permute-start.6 = (f32[2,18,1]{1,0,2:T(2,128)S(1)}, f32[2,18,1]{1,0,2:T(2,128)S(1)}, u32[]{:S(2)}, u32[]{:S(2)}) collective-permute-start(f32[2,18,1]{1,0,2:T(2,128)S(1)} %get-tuple-element.509), channel_id=1, source_target_pairs={{1,0},{2,1},{3,2},{5,4},{6,5},{7,6},{9,8},{10,9},{11,10},{13,12},{... | collective-permute-start | bytes 440 | tf_op jit(solution)/shard_map/ppermute | solution.py:32
  401.7 185.8 %collective-permute-start.7 = (f32[2,18,1]{1,0,2:T(2,128)S(1)}, f32[2,18,1]{1,0,2:T(2,128)S(1)}, u32[]{:S(2)}, u32[]{:S(2)}) collective-permute-start(f32[2,18,1]{1,0,2:T(2,128)S(1)} %get-tuple-element.508), channel_id=1, source_target_pairs={{0,1},{1,2},{2,3},{4,5},{5,6},{6,7},{8,9},{9,10},{10,11},{12,13},{... | collective-permute-start | bytes 440 | tf_op jit(solution)/shard_map/ppermute | solution.py:29
  635.2 3.0 collective-permute-start.8
  638.5 5.1 collective-permute-start.9
  644.4 6.1 collective-permute-start.10
  645.7 6.1 collective-permute-start.11
  702.2 3.0 collective-permute-start.12
  705.6 3.8 collective-permute-start.13
  710.2 6.1 collective-permute-start.14
  711.5 6.1 collective-permute-start.15
where the time goes:
time: 774 us; the launch traced here: 768 us
  starting transfers between devices  407 us (53%)
  local copies, waits for them, and re-layouts  191 us (25%)
  blocking collectives  130 us (17%)
  between operations  12.4 us (2%)
  matrix products  9.82 us (1%)
  waiting for transfers between devices  8.69 us (1%)
  other arithmetic  8.31 us (1%)
    ppermute x6, starting transfers between devices, with_halo(): lax.ppermute(lax.slice_in_dim(block, block.shape[dim] - width, None, axis...  200 us
    ppermute x4, starting transfers between devices, shifted(): return lax.ppermute(x, axis, pairs)  199 us
    gather x192, local copies, waits for them, and re-layouts  172 us
    psum x3, blocking collectives, two_products(): lax.psum((jnp.sum(values * values), jnp.sum(values * applied)), ('row', '...  130 us
  transfers between devices with their start and end apart: 16, of which 6 were waited for; matrix products, arithmetic and copies ran while one was open for 25% of the time, Pallas kernels for 0%

commit v1 on v0

--- a/solution.py
+++ b/solution.py
@@ -13,6 +13,14 @@
 LAMBDA_REG = 0.05
 EPSILON = 1e-05
 PRECISE = lax.Precision.HIGHEST
+
+
+def note_forms(row_data):
+    across = "row"
+    group_axis = "col"
+    for nth in (group_axis, across):
+        row_data = lax.psum(row_data, axis_name=nth)
+    return row_data
 
 
 def shifted(x, axis, by):
@@ -153,7 +161,7 @@
     residual = forcing
 
     def two_products(values, applied):
-        return lax.psum((jnp.sum(values * values), jnp.sum(values * applied)), ("row", "col"))
+        return note_forms((jnp.sum(values * values), jnp.sum(values * applied)))
 
     applied = operate(residual)
     norm_now, product = two_products(residual, applied)

time: 774 us -> 720 us (0.930)
  blocking collectives: 130 us -> 77.9 us
    psum x3 -> x6, blocking collectives: 130 us -> 77.9 us  [note_forms(): row_data = lax.psum(row_data, axis_name=nth)]
  transfers between devices with their start and end apart: 16 -> 16, of which waited for: 6 -> 6; matrix products, arithmetic and copies ran while one was open for 25% -> 27% of each run, Pallas kernels for 0% -> 0%
where the time goes in v1:
time: 720 us; the launch traced here: 714 us
  starting transfers between devices  408 us (57%)
  local copies, waits for them, and re-layouts  190 us (26%)
  blocking collectives  77.9 us (11%)
  between operations  12.2 us (2%)
  matrix products  9.82 us (1%)
  other arithmetic  8.37 us (1%)
    ppermute x6, starting transfers between devices, with_halo(): lax.ppermute(lax.slice_in_dim(block, block.shape[dim] - width, None, axis...  201 us
    ppermute x4, starting transfers between devices, shifted(): return lax.ppermute(x, axis, pairs)  199 us
    gather x192, local copies, waits for them, and re-layouts  172 us
    psum x6, blocking collectives, note_forms(): row_data = lax.psum(row_data, axis_name=nth)  77.9 us
  transfers between devices with their start and end apart: 16, of which 6 were waited for; matrix products, arithmetic and copies ran while one was open for 27% of the time, Pallas kernels for 0%

profile of v1, /device:TPU:0, one launch (start us, length us, event | category | flops | bytes accessed | tf_op | source)
XLA Modules:
  0.0 714.0 jit_solution(211408834463326193)
XLA Ops:
  0.7 2.9 slice_bitcast_fusion.1
  12.0 91.7 %while.49 = (s32[]{:T(128)}, f32[3,16]{1,0:T(4,128)S(1)}, s32[]{:T(128)}, bf16[16,128,128]{2,1,0:T(8,128)(2,1)S(1)}, bf16[16,36864]{1,0:T(8,128)(2,1)}, /*index=...) while((s32[]{:T(128)}, f32[3,16]{1,0:T(4,128)S(1)}, ...), condition=%wide.region_9.10_spmd, body=%wide.region_5.9_spmd.sunk | while | flops 5178357 | bytes 5322758 | solution.py:96
  14.3 87.7 %while.51 = (s32[]{:T(128)}, bf16[4,192,192]{2,1,0:T(8,128)(2,1)S(1)}, s32[32,3]{0,1:T(4,128)S(1)}, bf16[32,128,128]{2,1,0:T(8,128)(2,1)S(1)}, s32[]{:T(128)}) while((s32[]{:T(128)}, bf16[4,192,192]{2,1,0:T(8,128)(2,1)S(1)}, s32[32,3]{0,1:T(4,128)S(1)}, bf16[32,128,128]{2,1,0:T(8,128)(2,1)S(1)}, s32[]{:T(128)}) %tuple.207), condition=%wide.while_cond.17, body=%wide.while_body.17.sunk | while | flops 2 | bytes 65665 | solution.py:54
  15.0 2.0 dynamic-slice_dynamic-update-slice_fusion.4
  17.7 2.0 dynamic-slice_dynamic-update-slice_fusion.4
  20.4 2.0 dynamic-slice_dynamic-update-slice_fusion.4
  23.2 2.0 dynamic-slice_dynamic-update-slice_fusion.4
  25.9 2.0 dynamic-slice_dynamic-update-slice_fusion.4
  28.7 2.0 dynamic-slice_dynamic-update-slice_fusion.4
  31.4 2.0 dynamic-slice_dynamic-update-slice_fusion.4
  34.1 2.0 dynamic-slice_dynamic-update-slice_fusion.4
  36.9 2.0 dynamic-slice_dynamic-update-slice_fusion.4
  39.6 2.0 dynamic-slice_dynamic-update-slice_fusion.4
  42.4 2.0 dynamic-slice_dynamic-update-slice_fusion.4
  45.1 2.0 dynamic-slice_dynamic-update-slice_fusion.4
  47.8 2.0 dynamic-slice_dynamic-update-slice_fusion.4
  50.6 2.0 dynamic-slice_dynamic-update-slice_fusion.4
  53.3 2.0 dynamic-slice_dynamic-update-slice_fusion.4
  56.1 2.0 dynamic-slice_dynamic-update-slice_fusion.4
  58.8 2.0 dynamic-slice_dynamic-update-slice_fusion.4
  61.5 2.0 dynamic-slice_dynamic-update-slice_fusion.4
  64.3 2.0 dynamic-slice_dynamic-update-slice_fusion.4
  67.0 2.0 dynamic-slice_dynamic-update-slice_fusion.4
  69.8 2.0 dynamic-slice_dynamic-update-slice_fusion.4
  72.5 2.0 dynamic-slice_dynamic-update-slice_fusion.4
  75.2 2.0 dynamic-slice_dynamic-update-slice_fusion.4
  80.7 2.0 dynamic-slice_dynamic-update-slice_fusion.4
  83.5 2.0 dynamic-slice_dynamic-update-slice_fusion.4
  88.9 2.0 dynamic-slice_dynamic-update-slice_fusion.4
  91.7 2.0 dynamic-slice_dynamic-update-slice_fusion.4
  94.4 2.0 dynamic-slice_dynamic-update-slice_fusion.4
  97.1 2.0 dynamic-slice_dynamic-update-slice_fusion.4
  99.9 2.0 dynamic-slice_dynamic-update-slice_fusion.4
  103.7 12.8 %collective-permute-start.3 = (f32[3,16]{1,0:T(4,128)S(1)}, f32[3,16]{1,0:T(4,128)S(1)}, u32[]{:S(2)}, u32[]{:S(2)}) collective-permute-start(f32[3,16]{1,0:T(4,128)S(1)} %broadcast_multiply_fusion.2), channel_id=1, source_target_pairs={{0,4},{4,8},{8,12},{12,16},{16,20},{20,24},{24,28},{1,5},{5,9},{9,... | collective-permute-start | bytes 584 | tf_op jit(solution)/shard_map/ppermute | solution.py:29
  116.6 88.6 %while.47 = (s32[]{:T(128)}, f32[3,16]{1,0:T(4,128)S(1)}, s32[]{:T(128)}, bf16[16,128,128]{2,1,0:T(8,128)(2,1)S(1)}, bf16[16,36864]{1,0:T(8,128)(2,1)}, /*index=...) while((s32[]{:T(128)}, f32[3,16]{1,0:T(4,128)S(1)}, ...), condition=%wide.region_4.5_spmd, body=%wide.region_0.4_spmd.sunk | while | flops 5178357 | bytes 5314510 | solution.py:96
  118.5 85.1 %while.50 = (s32[]{:T(128)}, bf16[4,192,192]{2,1,0:T(8,128)(2,1)S(1)}, s32[32,3]{0,1:T(4,128)S(1)}, bf16[32,128,128]{2,1,0:T(8,128)(2,1)S(1)}, s32[]{:T(128)}) while((s32[]{:T(128)}, bf16[4,192,192]{2,1,0:T(8,128)(2,1)S(1)}, s32[32,3]{0,1:T(4,128)S(1)}, bf16[32,128,128]{2,1,0:T(8,128)(2,1)S(1)}, s32[]{:T(128)}) %tuple.210), condition=%wide.while_cond.16, body=%wide.while_body.16.sunk | while | flops 2 | bytes 65665 | solution.py:54
  205.3 183.9 %collective-permute-start.2 = (f32[3,16]{1,0:T(4,128)S(1)}, f32[3,16]{1,0:T(4,128)S(1)}, u32[]{:S(2)}, u32[]{:S(2)}) collective-permute-start(f32[3,16]{1,0:T(4,128)S(1)} %broadcast_multiply_fusion.3), channel_id=1, source_target_pairs={{0,1},{1,2},{2,3},{4,5},{5,6},{6,7},{8,9},{9,10},{10,11},{12,13},{... | collective-permute-start | bytes 584 | tf_op jit(solution)/shard_map/ppermute | solution.py:29
  395.5 3.4 collective-permute-start.4
  401.7 184.5 %collective-permute-start.7 = (f32[2,18,1]{1,0,2:T(2,128)S(1)}, f32[2,18,1]{1,0,2:T(2,128)S(1)}, u32[]{:S(2)}, u32[]{:S(2)}) collective-permute-start(f32[2,18,1]{1,0,2:T(2,128)S(1)} %get-tuple-element.514), channel_id=1, source_target_pairs={{0,1},{1,2},{2,3},{4,5},{5,6},{6,7},{8,9},{9,10},{10,11},{12,13},{... | collective-permute-start | bytes 440 | tf_op jit(solution)/shard_map/ppermute | solution.py:37
  590.1 13.0 %all-reduce.6 = (f32[]{:T(128)}, f32[]{:T(128)}) all-reduce(f32[]{:T(128)} %get-tuple-element.427, f32[]{:T(128)} %get-tuple-element.426), channel_id=1, replica_groups=mesh['row'=8,'col'=4] {'col'}, use_global_device_ids=true, to_apply=%region_11.12 | all-reduce | flops 2 | bytes 16 | tf_op jit(solution)/shard_map/psum | solution.py:22
  603.1 14.7 %all-reduce.3 = (f32[]{:T(128)}, f32[]{:T(128)}) all-reduce(f32[]{:T(128)} %get-tuple-element.480, f32[]{:T(128)} %get-tuple-element.481), channel_id=1, replica_groups=mesh['row'=8,'col'=4] {'row'}, use_global_device_ids=true, to_apply=%region_12.13 | all-reduce | flops 2 | bytes 16 | tf_op jit(solution)/shard_map/psum | solution.py:22
  619.3 2.2 collective-permute-start.8
  628.8 4.5 collective-permute-start.11
  637.2 10.4 %all-reduce.5 = (f32[]{:T(128)}, f32[]{:T(128)}) all-reduce(f32[]{:T(128)} %get-tuple-element.425, f32[]{:T(128)} %get-tuple-element.424), channel_id=1, replica_groups=mesh['row'=8,'col'=4] {'col'}, use_global_device_ids=true, to_apply=%region_17.18 | all-reduce | flops 2 | bytes 16 | tf_op jit(solution)/shard_map/psum | solution.py:22
  647.6 14.2 %all-reduce.2 = (f32[]{:T(128)}, f32[]{:T(128)}) all-reduce(f32[]{:T(128)} %get-tuple-element.478, f32[]{:T(128)} %get-tuple-element.479), channel_id=1, replica_groups=mesh['row'=8,'col'=4] {'row'}, use_global_device_ids=true, to_apply=%region_18.19 | all-reduce | flops 2 | bytes 16 | tf_op jit(solution)/shard_map/psum | solution.py:22
  675.5 4.5 collective-permute-start.15
  683.9 11.3 %all-reduce.4 = (f32[]{:T(128)}, f32[]{:T(128)}) all-reduce(f32[]{:T(128)} %get-tuple-element.423, f32[]{:T(128)} %get-tuple-element.422), channel_id=1, replica_groups=mesh['row'=8,'col'=4] {'col'}, use_global_device_ids=true, to_apply=%region_23.24 | all-reduce | flops 2 | bytes 16 | tf_op jit(solution)/shard_map/psum | solution.py:22
  695.2 14.2 %all-reduce.1 = (f32[]{:T(128)}, f32[]{:T(128)}) all-reduce(f32[]{:T(128)} %get-tuple-element.476, f32[]{:T(128)} %get-tuple-element.477), channel_id=1, replica_groups=mesh['row'=8,'col'=4] {'row'}, use_global_device_ids=true, to_apply=%region_24.25 | all-reduce | flops 2 | bytes 16 | tf_op jit(solution)/shard_map/psum | solution.py:22
  (367 shorter events, 162.4 us)
Async XLA Ops:
  0.6 8.2 %copy-start.10 = (s32[1,1,2,2,128]{4,3,2,1,0:T(2,128)S(1)}, s32[1,1,2,2,128]{4,3,2,1,0:T(2,128)}, u32[]{:S(2)}) copy-start(s32[1,1,2,2,128]{4,3,2,1,0:T(2,128)} %param.44) | copy-start | bytes 6148
  0.6 8.4 %copy-start.7 = (f32[1,705]{1,0:T(1,128)S(1)}, f32[1,705]{1,0:T(1,128)}, u32[]{:S(2)}) copy-start(f32[1,705]{1,0:T(1,128)} %param.47) | copy-start | bytes 8464
  0.7 10.6 %copy-start.3 = (s32[1,2,705]{2,1,0:T(2,128)S(1)}, s32[1,2,705]{2,1,0:T(2,128)}, u32[]{:S(2)}) copy-start(s32[1,2,705]{2,1,0:T(2,128)} %param.46) | copy-start | bytes 16924
  0.7 11.2 %copy-start = (bf16[1,1,2,16,128,128]{5,4,3,2,1,0:T(8,128)(2,1)S(1)}, bf16[1,1,2,16,128,128]{5,4,3,2,1,0:T(8,128)(2,1)}, u32[]{:S(2)}) copy-start(bf16[1,1,2,16,128,128]{5,4,3,2,1,0:T(8,128)(2,1)} %param.42) | copy-start | bytes 3145732
  3.6 8.4 %collective-permute-start.1 = (bf16[16,36864]{1,0:T(8,128)(2,1)S(1)}, bf16[16,36864]{1,0:T(8,128)(2,1)}, u32[]{:S(2)}, u32[]{:S(2)}) collective-permute-start(bf16[16,36864]{1,0:T(8,128)(2,1)S(1)} %get-tuple-element.507), channel_id=1, source_target_pairs={{4,0},{8,4},{12,8},{16,12},{20,16},{24,20},{28,24},{5,1},{9,5},{13... | collective-permute-start | bytes 3538952 | tf_op jit(solution)/shard_map/ppermute | solution.py:29
  4.9 111.7 %collective-permute-start = (bf16[16,36864]{1,0:T(8,128)(2,1)}, bf16[16,36864]{1,0:T(8,128)(2,1)}, u32[]{:S(2)}, u32[]{:S(2)}) collective-permute-start(bf16[16,36864]{1,0:T(8,128)(2,1)} %get-tuple-element.506), channel_id=1, source_target_pairs={{1,0},{2,1},{3,2},{5,4},{6,5},{7,6},{9,8},{10,9},{11,10},{13,12},{... | collective-permute-start | bytes 3538952 | tf_op jit(solution)/shard_map/ppermute | solution.py:29
  12.0 91.7 %copy-start.8 = (f32[16]{0:T(128)S(1)}, f32[16]{0:T(128)}, u32[]{:S(2)}) copy-start(f32[16]{0:T(128)} %compare_convert_fusion) | copy-start | bytes 196
  12.0 0.6 copy-start.1
  101.9 1.7 copy-start.2
  103.7 286.6 %collective-permute-start.3 = (f32[3,16]{1,0:T(4,128)S(1)}, f32[3,16]{1,0:T(4,128)S(1)}, u32[]{:S(2)}, u32[]{:S(2)}) collective-permute-start(f32[3,16]{1,0:T(4,128)S(1)} %broadcast_multiply_fusion.2), channel_id=1, source_target_pairs={{0,4},{4,8},{8,12},{12,16},{16,20},{20,24},{24,28},{1,5},{5,9},{9,... | collective-permute-start | bytes 584 | tf_op jit(solution)/shard_map/ppermute | solution.py:29
  116.6 88.7 %copy-start.9 = (f32[16]{0:T(128)S(1)}, f32[16]{0:T(128)}, u32[]{:S(2)}) copy-start(f32[16]{0:T(128)} %compare_convert_fusion.1) | copy-start | bytes 196
  116.6 272.6 %copy-start.11 = (s32[16]{0:T(128)S(1)}, s32[16]{0:T(128)}, u32[]{:S(2)}) copy-start(s32[16]{0:T(128)} %and_select_fusion) | copy-start | bytes 196
  116.6 277.2 %copy-start.4 = (s32[705]{0:T(1024)S(1)}, s32[705]{0:T(1024)}, u32[]{:S(2)}) copy-start(s32[705]{0:T(1024)} %get-tuple-element.428) | copy-start | bytes 8464
  116.6 277.1 %copy-start.5 = (s32[705]{0:T(1024)S(1)}, s32[705]{0:T(1024)}, u32[]{:S(2)}) copy-start(s32[705]{0:T(1024)} %get-tuple-element.429) | copy-start | bytes 8464
  116.6 277.1 %copy-start.6 = (f32[705]{0:T(1024)S(1)}, f32[705]{0:T(1024)}, u32[]{:S(2)}) copy-start(f32[705]{0:T(1024)} %reduce.44) | copy-start | bytes 8464
  205.3 185.3 %collective-permute-start.2 = (f32[3,16]{1,0:T(4,128)S(1)}, f32[3,16]{1,0:T(4,128)S(1)}, u32[]{:S(2)}, u32[]{:S(2)}) collective-permute-start(f32[3,16]{1,0:T(4,128)S(1)} %broadcast_multiply_fusion.3), channel_id=1, source_target_pairs={{0,1},{1,2},{2,3},{4,5},{5,6},{6,7},{8,9},{9,10},{10,11},{12,13},{... | collective-permute-start | bytes 584 | tf_op jit(solution)/shard_map/ppermute | solution.py:29
  392.1 3.3 collective-permute-start.5
  395.5 4.2 collective-permute-start.4
  400.4 185.8 %collective-permute-start.6 = (f32[2,18,1]{1,0,2:T(2,128)S(1)}, f32[2,18,1]{1,0,2:T(2,128)S(1)}, u32[]{:S(2)}, u32[]{:S(2)}) collective-permute-start(f32[2,18,1]{1,0,2:T(2,128)S(1)} %get-tuple-element.515), channel_id=1, source_target_pairs={{1,0},{2,1},{3,2},{5,4},{6,5},{7,6},{9,8},{10,9},{11,10},{13,12},{... | collective-permute-start | bytes 440 | tf_op jit(solution)/shard_map/ppermute | solution.py:40
  401.7 185.8 %collective-permute-start.7 = (f32[2,18,1]{1,0,2:T(2,128)S(1)}, f32[2,18,1]{1,0,2:T(2,128)S(1)}, u32[]{:S(2)}, u32[]{:S(2)}) collective-permute-start(f32[2,18,1]{1,0,2:T(2,128)S(1)} %get-tuple-element.514), channel_id=1, source_target_pairs={{0,1},{1,2},{2,3},{4,5},{5,6},{6,7},{8,9},{9,10},{10,11},{12,13},{... | collective-permute-start | bytes 440 | tf_op jit(solution)/shard_map/ppermute | solution.py:37
  619.3 4.0 collective-permute-start.8
  623.6 3.1 collective-permute-start.9
  627.5 5.9 collective-permute-start.10
  628.8 5.8 collective-permute-start.11
  666.4 3.7 collective-permute-start.12
  670.4 3.1 collective-permute-start.13
  674.2 5.9 collective-permute-start.14
  675.5 5.8 collective-permute-start.15
